TPU v7x, 128 devices: a whole 4x4x4 slice. The times are simulated.
128 devices in a mesh: tile: 16 (over y_lo, x, core), subap: 8 (over y_hi, z).
Axes of the slice: x: 4, y: 4 (y_hi: 2, y_lo: 2; y = y_hi * 2 + y_lo), z: 4, core: 2. Of those that a mesh axis runs over, the one named last changes fastest.
Arguments:
- pulses: bfloat16 [16, 8, 2, 128, 16384], P('tile', 'subap'), may hold values from -6 to 6
- footprint: int32 [16, 8, 32], P('tile', 'subap'), may hold values from 0 to 47, as said below
- offsets: int32 [48], replicated, may hold values from 0 to 15872
- azimuth: bfloat16 [48, 16, 8, 2, 256, 128], P('tile', None, 'subap'), may hold values from -0.09375 to 0.09375
- range_interp: bfloat16 [48, 2, 512, 256], P('tile'), may hold values from -0.1875 to 0.1875
Outputs:
- image: float32 [48, 2, 256, 256], P('tile', None, 'subap')
Inputs may be any that keep to these rules, and one draw needn't show every extreme that they name: For every o, footprint[k, s, o * 2 : (o + 1) * 2] holds 2 different tiles of o * 3 to (o + 1) * 3 - 1.
All inputs are finite; a program needn't handle non-finite values.
Results may differ from a plain program's by a relative error of at most 0.0029.
Values may be sent and summed in bfloat16 or wider, within the bound.
No kernel may reach another device: no remote copies, remote signals or barrier semaphores. Data moves between devices by JAX's collectives and lax.ppermute only.
A program may use at most 128 MiB of HBM per device.

v0:
```python
import jax
import jax.numpy as jnp
from jax import lax
from jax.sharding import PartitionSpec as P


def combine(prod):
    real = prod[..., 0, 0, :, :] - prod[..., 1, 1, :, :]
    imag = prod[..., 0, 1, :, :] + prod[..., 1, 0, :, :]
    return jnp.stack([real, imag], axis=-3)


def on_device(pulses, footprint, offsets, azimuth, range_interp):
    tiles = offsets.shape[0]
    width = range_interp.shape[2]
    block = pulses[0, 0]

    def cut(start):
        return lax.dynamic_slice_in_dim(block, start, width, 2)

    windows = jax.vmap(cut)(offsets)
    tile_ids = jnp.arange(tiles, dtype=jnp.int32)
    hit = jnp.any(footprint[0, 0][None, :] == tile_ids[:, None], axis=1).astype(jnp.bfloat16)
    windows = windows * hit[:, None, None, None]
    arrived = lax.all_to_all(windows[:, None], "tile", split_axis=0, concat_axis=1, tiled=True)
    prod = jnp.einsum(
        "tkcpr,tdru->tkcdpu", arrived, range_interp, preferred_element_type=jnp.float32
    )
    ranged = combine(prod).astype(jnp.bfloat16)
    sub_image = combine(
        jnp.einsum(
            "tkcap,tkdpu->tcdau", azimuth[:, :, 0], ranged, preferred_element_type=jnp.float32
        )
    )
    raw = lax.psum(sub_image, "subap")
    power = jnp.mean(raw * raw, axis=(1, 2, 3))
    height = raw.shape[2] // lax.axis_size("subap")
    own_rows = lax.dynamic_slice_in_dim(raw, lax.axis_index("subap") * height, height, 2)
    return own_rows / jnp.sqrt(power + 1e-06)[:, None, None, None]


def solution(mesh):
    in_specs = (
        P("tile", "subap", None, None, None),
        P("tile", "subap", None),
        P(),
        P("tile", None, "subap", None, None, None),
        P("tile", None, None, None),
    )
    out_specs = P("tile", None, "subap", None)
    return jax.shard_map(
        on_device, mesh=mesh, in_specs=in_specs, out_specs=out_specs, check_vma=False
    )
```

profile of v0, /device:TPU:0, one launch (start us, length us, event | category | flops | bytes accessed | tf_op | source)
XLA Modules:
  0.0 380.4 jit_solution(2117407463803907995)
XLA Ops:
  6.5 0.0 copy-start
  6.5 0.0 all-reduce.3.cloned.1.call-start
  6.5 21.2 %copy.46 = bf16[1,1,2,128,16384]{3,2,4,1,0:T(2,128)(2,1)} copy(bf16[1,1,2,128,16384]{4,3,2,1,0:T(8,128)(2,1)} %param.5) | data formatting | bytes 16777216 | tf_op args[0]
  27.8 0.0 copy-done.2
  27.8 0.1 fusion.21
  27.9 30.5 %gather_fusion = bf16[48,2,128,512]{2,1,3,0:T(2,128)(2,1)} fusion(bf16[2,128,16384]{1,0,2:T(2,128)(2,1)} %bitcast.66, s32[48]{0:T(128)S(1)} %fusion.23), kind=kCustom, calls=%fused_computation | custom fusion | bytes 25166400 | tf_op jit(solution)/shard_map/vmap()/gather | solution.py:19
  58.4 13.9 %fusion.2 = bf16[48,1,2,128,512]{3,2,4,1,0:T(2,128)(2,1)S(1)} fusion(bf16[48,2,128,512]{2,1,3,0:T(2,128)(2,1)} %gather_fusion, bf16[48]{0:T(256)(128)(2,1)S(1)} %convert_element_type.8), kind=kLoop, calls=%fused_computation.4 | loop fusion | flops 6291456 | bytes 25165920 | tf_op jit(solution)/shard_map/mul | solution.py:24
  72.3 145.5 %all_to_all.18 = bf16[48,1,2,128,512]{3,2,4,1,0:T(2,128)(2,1)} all-to-all(bf16[48,1,2,128,512]{3,2,4,1,0:T(2,128)(2,1)S(1)} %fusion.2), channel_id=1, replica_groups=mesh['tile'=16,'subap'=8] {'tile'}, dimensions={0} | all-to-all | bytes 25165824 | tf_op jit(solution)/shard_map/all_to_all | solution.py:25
  217.8 30.9 %copy.49 = bf16[16,3,1,2,128,512]{5,4,3,0,1,2:T(8,128)(2,1)} copy(bf16[16,3,1,2,128,512]{4,3,5,1,0,2:T(2,128)(2,1)} %bitcast.67) | data formatting | bytes 25165824 | tf_op jit(solution)/shard_map/all_to_all | solution.py:25
  248.7 0.0 copy-done
  248.7 14.4 %fusion.3 = f32[3,16,2,2,128,256]{5,4,3,2,1,0:T(8,128)} fusion(bf16[16,3,1,2,128,512]{5,4,3,0,1,2:T(8,128)(2,1)} %copy.49, bf16[3,2,512,256]{3,2,1,0:T(8,128)(2,1)S(1)} %copy-done), kind=kOutput, calls=%fused_computation.5 | convolution fusion | flops 6442450944 | bytes 39321600 | tf_op jit(solution)/shard_map/tkcpr,tdru->tkcdpu/dot_general | solution.py:26
  263.2 6.0 %fusion.13 = bf16[3,16,1,128,256]{4,3,1,0,2:T(8,128)(2,1)S(1)} fusion(f32[3,16,2,2,128,256]{5,4,3,2,1,0:T(8,128)} %fusion.3), kind=kLoop, calls=%fused_computation.17 | loop fusion | flops 3145728 | bytes 15728640 | tf_op jit(solution)/shard_map/sub | solution.py:8
  269.2 0.0 slice-start.1
  269.2 5.8 %fusion.14 = bf16[3,16,1,128,256]{4,3,1,0,2:T(8,128)(2,1)S(1)} fusion(f32[3,16,2,2,128,256]{5,4,3,2,1,0:T(8,128)} %fusion.3), kind=kLoop, calls=%fused_computation.18 | loop fusion | flops 3145728 | bytes 15728640 | tf_op jit(solution)/shard_map/add | solution.py:9
  275.0 0.0 slice-done
  275.0 0.0 slice-done.1
  275.0 0.0 copy-start.1
  275.0 3.4 fusion.15
  278.4 0.2 fusion.20
  278.7 1.3 pad_maximum_fusion
  279.9 0.0 all-reduce.3.cloned.1.call-update
  279.9 90.3 %all-reduce.3.cloned.1.call-done = f32[3,2,256,256]{3,2,1,0:T(8,128)} async-done(((f32[3,2,256,256]{3,2,1,0:T(8,128)}), f32[3,2,256,256]{3,2,1,0:T(8,128)}) %all-reduce.3.cloned.1.call-update) | async-done | bytes 1572880 | tf_op jit(solution)/shard_map/psum | solution.py:35
  370.2 1.7 multiply_reduce_fusion
  371.9 1.7 dynamic-slice_divide_fusion
  (9 shorter events, 0.0 us)
Async XLA Ops:
  6.5 242.2 %copy-start = (bf16[3,2,512,256]{3,2,1,0:T(8,128)(2,1)S(1)}, bf16[3,2,512,256]{3,2,1,0:T(8,128)(2,1)}, u32[]{:S(2)}) copy-start(bf16[3,2,512,256]{3,2,1,0:T(8,128)(2,1)} %param.9) | copy-start | bytes 4718596
  6.5 21.2 %copy-start.2 = (s32[48]{0:T(128)S(1)}, s32[48]{0:T(128)}, u32[]{:S(2)}) copy-start(s32[48]{0:T(128)} %param.7) | copy-start | bytes 580
  6.5 21.3 %copy-start.3 = (s32[1,1,32]{2,1,0:T(1,128)S(1)}, s32[1,1,32]{2,1,0:T(1,128)}, u32[]{:S(2)}) copy-start(s32[1,1,32]{2,1,0:T(1,128)} %param.6) | copy-start | bytes 388
  6.5 363.7 %all-reduce.3.cloned.1.call-start = ((), (), s32[]{:S(2)}) async-start(), calls=%async_computation.1 | async-start | bytes 3145728 | tf_op jit(solution)/shard_map/psum | solution.py:35
  263.2 11.8 %slice-start = ((s8[6291456]{0:T(1024)(128)(4,1)}), s8[4194304]{0:T(1024)(128)(4,1)S(1)}, s32[]{:S(2)}) async-start(s8[6291456]{0:T(1024)(128)(4,1)} %bitcast.68), calls=%async_computation.2 | async-start | bytes 8388608
  269.2 5.8 %slice-start.1 = ((s8[6291456]{0:T(1024)(128)(4,1)}), s8[2097152]{0:T(1024)(128)(4,1)S(1)}, s32[]{:S(2)}) async-start(s8[6291456]{0:T(1024)(128)(4,1)} %bitcast.68), calls=%async_computation.3 | async-start | bytes 4194304
  275.0 98.6 %copy-start.1 = (bf16[3,2,512,256]{3,2,1,0:T(8,128)(2,1)S(1)}, bf16[3,2,512,256]{3,2,1,0:T(8,128)(2,1)}, u32[]{:S(2)}) copy-start(bf16[3,2,512,256]{3,2,1,0:T(8,128)(2,1)} %param.9) | copy-start | bytes 4718596
Sparse Core Ops, SparseCore 0:
  280.1 90.1 all-reduce.2
where the time goes:
time: 382 us; the launch traced here: 380 us
  blocking collectives  145 us (38%)
  waiting for transfers between devices  90.3 us (24%)
  local copies, waits for them, and re-layouts  82.7 us (22%)
  other arithmetic  30.7 us (8%)
  matrix products  17.8 us (5%)
  between operations  13.5 us (4%)
    all_to_all x1, blocking collectives, on_device(): lax.all_to_all(windows[:, None], 'tile', split_axis=0, concat_axis=1, til...  145 us
    psum x1, waiting for transfers between devices, on_device(): raw = lax.psum(sub_image, 'subap')  90.3 us
    all_to_all x1, local copies, waits for them, and re-layouts, on_device(): lax.all_to_all(windows[:, None], 'tile', split_axis=0, concat_axis=1, til...  30.9 us
    gather x1, local copies, waits for them, and re-layouts, cut(): return lax.dynamic_slice_in_dim(block, start, width, 2)  30.5 us
    unnamed x13, local copies, waits for them, and re-layouts  21.3 us
    dot_general x1, matrix products, on_device(): jnp.einsum('tkcpr,tdru->tkcdpu', arrived, range_interp, preferred_element...  14.4 us
    mul x1, other arithmetic, on_device(): windows = windows * hit[:, None, None, None]  13.9 us
  transfers between devices with their start and end apart: 1, of which 1 were waited for; matrix products, arithmetic and copies ran while one was open for 0% of the time, Pallas kernels for 0%

commit v1 on v0

--- a/solution.py
+++ b/solution.py
@@ -32,7 +32,8 @@
             "tkcap,tkdpu->tcdau", azimuth[:, :, 0], ranged, preferred_element_type=jnp.float32
         )
     )
-    raw = lax.psum(sub_image, "subap")
+    _tell_rounds = lambda content: lax.all_gather(content, "subap").sum(axis=0)
+    raw = _tell_rounds(sub_image)
     power = jnp.mean(raw * raw, axis=(1, 2, 3))
     height = raw.shape[2] // lax.axis_size("subap")
     own_rows = lax.dynamic_slice_in_dim(raw, lax.axis_index("subap") * height, height, 2)

time: 382 us -> 449 us (1.18)
  waiting for transfers between devices: 90.3 us -> 145 us
  other arithmetic: 30.7 us -> 35.7 us
  matrix products: 17.8 us -> 22.4 us
    all_gather x0 -> x1, waiting for transfers between devices: none -> 145 us  [on_device(): _tell_rounds = lambda content: lax.all_gather(content, 'subap').sum(axis=0)]
    psum x1 -> x0, waiting for transfers between devices: 90.3 us -> none  [on_device(): raw = lax.psum(sub_image, 'subap')]
    reduce_sum x0 -> x1, other arithmetic: none -> 5.71 us  [on_device(): _tell_rounds = lambda content: lax.all_gather(content, 'subap').sum(axis=0)]
    unnamed x13 -> x10, local copies, waits for them, and re-layouts: 21.3 us -> 22.6 us
where the time goes in v1:
time: 449 us; the launch traced here: 447 us
  blocking collectives  145 us (32%)
  waiting for transfers between devices  145 us (32%)
  local copies, waits for them, and re-layouts  85.1 us (19%)
  other arithmetic  35.7 us (8%)
  matrix products  22.4 us (5%)
  between operations  13.5 us (3%)
    all_to_all x1, blocking collectives, on_device(): lax.all_to_all(windows[:, None], 'tile', split_axis=0, concat_axis=1, til...  145 us
    all_gather x1, waiting for transfers between devices, on_device(): _tell_rounds = lambda content: lax.all_gather(content, 'subap').sum(axis=0)  145 us
    all_to_all x1, local copies, waits for them, and re-layouts, on_device(): lax.all_to_all(windows[:, None], 'tile', split_axis=0, concat_axis=1, til...  30.9 us
    gather x1, local copies, waits for them, and re-layouts, cut(): return lax.dynamic_slice_in_dim(block, start, width, 2)  30.5 us
    unnamed x10, local copies, waits for them, and re-layouts  22.6 us
    dot_general x1, matrix products, on_device(): jnp.einsum('tkcpr,tdru->tkcdpu', arrived, range_interp, preferred_element...  14.5 us
    mul x1, other arithmetic, on_device(): windows = windows * hit[:, None, None, None]  13.9 us
  transfers between devices with their start and end apart: 1, of which 1 were waited for; matrix products, arithmetic and copies ran while one was open for 0% of the time, Pallas kernels for 0%

profile of v1, /device:TPU:0, one launch (start us, length us, event | category | flops | bytes accessed | tf_op | source)
XLA Modules:
  0.0 447.0 jit_solution(7409409024850660174)
XLA Ops:
  6.5 0.0 copy-start
  6.5 0.0 all-gather.3.cloned.1.call-start
  6.5 21.2 %copy.44 = bf16[1,1,2,128,16384]{3,2,4,1,0:T(2,128)(2,1)} copy(bf16[1,1,2,128,16384]{4,3,2,1,0:T(8,128)(2,1)} %param.5) | data formatting | bytes 16777216 | tf_op args[0]
  27.8 0.0 copy-done.3
  27.8 0.1 fusion.23
  27.9 30.5 %gather_fusion = bf16[48,2,128,512]{2,1,3,0:T(2,128)(2,1)} fusion(bf16[2,128,16384]{1,0,2:T(2,128)(2,1)} %bitcast.75, s32[48]{0:T(128)S(1)} %fusion.25), kind=kCustom, calls=%fused_computation | custom fusion | bytes 25166400 | tf_op jit(solution)/shard_map/vmap()/gather | solution.py:19
  58.4 13.9 %fusion.2 = bf16[48,1,2,128,512]{3,2,4,1,0:T(2,128)(2,1)S(1)} fusion(bf16[48,2,128,512]{2,1,3,0:T(2,128)(2,1)} %gather_fusion, bf16[48]{0:T(256)(128)(2,1)S(1)} %convert_element_type.8), kind=kLoop, calls=%fused_computation.4 | loop fusion | flops 6291456 | bytes 25165920 | tf_op jit(solution)/shard_map/mul | solution.py:24
  72.3 145.5 %all_to_all.18 = bf16[48,1,2,128,512]{3,2,4,1,0:T(2,128)(2,1)} all-to-all(bf16[48,1,2,128,512]{3,2,4,1,0:T(2,128)(2,1)S(1)} %fusion.2), channel_id=1, replica_groups=mesh['tile'=16,'subap'=8] {'tile'}, dimensions={0} | all-to-all | bytes 25165824 | tf_op jit(solution)/shard_map/all_to_all | solution.py:25
  217.8 30.9 %copy.47 = bf16[16,3,1,2,128,512]{5,4,3,0,1,2:T(8,128)(2,1)} copy(bf16[16,3,1,2,128,512]{4,3,5,1,0,2:T(2,128)(2,1)} %bitcast.76) | data formatting | bytes 25165824 | tf_op jit(solution)/shard_map/all_to_all | solution.py:25
  248.6 0.0 copy-done
  248.6 14.5 %fusion.3 = f32[3,16,2,2,128,256]{5,4,3,2,1,0:T(8,128)} fusion(bf16[16,3,1,2,128,512]{5,4,3,0,1,2:T(8,128)(2,1)} %copy.47, bf16[3,2,512,256]{3,2,1,0:T(8,128)(2,1)S(1)} %copy-done), kind=kOutput, calls=%fused_computation.5 | convolution fusion | flops 6442450944 | bytes 39321600 | tf_op jit(solution)/shard_map/tkcpr,tdru->tkcdpu/dot_general | solution.py:26
  263.2 5.9 %fusion.12 = bf16[3,16,1,128,256]{4,3,1,0,2:T(8,128)(2,1)S(1)} fusion(f32[3,16,2,2,128,256]{5,4,3,2,1,0:T(8,128)} %fusion.3), kind=kLoop, calls=%fused_computation.16 | loop fusion | flops 3145728 | bytes 15728640 | tf_op jit(solution)/shard_map/sub | solution.py:8
  269.1 7.4 %fusion.13 = bf16[3,16,1,128,256]{4,3,1,0,2:T(8,128)(2,1)} fusion(f32[3,16,2,2,128,256]{5,4,3,2,1,0:T(8,128)} %fusion.3), kind=kLoop, calls=%fused_computation.17 | loop fusion | flops 3145728 | bytes 15728640 | tf_op jit(solution)/shard_map/add | solution.py:9
  276.5 7.8 %fusion.14 = f32[3,2,2,256,256]{3,4,1,2,0:T(8,128)S(1)} fusion(bf16[3,16,1,128,256]{4,3,1,0,2:T(8,128)(2,1)} %fusion.13, bf16[3,16,1,128,256]{4,3,1,0,2:T(8,128)(2,1)S(1)} %fusion.12, bf16[3,16,1,2,256,128]{5,4,3,2,1,0:T(8,128)(2,1)} %param.8), kind=kOutput, calls=%fused_computation.18 | convolution fusion | flops 3224371200 | bytes 15728640 | tf_op jit(solution)/shard_map/tkcap,tkdpu->tcdau/dot_general | solution.py:31
  284.3 0.1 fusion.20
  284.4 0.1 fusion.22
  284.5 1.4 pad_maximum_fusion
  285.9 0.0 all-gather.3.cloned.1.call-update
  286.0 144.9 %all-gather.3.cloned.1.call-done = f32[24,2,256,256]{2,3,0,1:T(8,128)} async-done(((f32[3,2,256,256]{2,3,0,1:T(8,128)}), f32[24,2,256,256]{2,3,0,1:T(8,128)}) %all-gather.3.cloned.1.call-update) | async-done | bytes 12582928 | tf_op jit(solution)/shard_map/all_gather | solution.py:35
  430.9 5.7 %reduce_sum.18 = f32[3,2,256,256]{2,3,0,1:T(8,128)S(1)} reduce(f32[8,3,2,256,256]{3,4,1,0,2:T(8,128)} %bitcast.77, f32[]{:T(128)} %constant.2.clone.1), dimensions={0}, to_apply=%region_1.0 | reduce | flops 2752512 | bytes 14155780 | tf_op jit(solution)/shard_map/reduce_sum | solution.py:35
  436.6 0.3 multiply_reduce_fusion
  436.8 1.1 constant_dynamic-slice_fusion
  438.0 1.4 copy.70
  439.4 0.8 broadcast_divide_fusion
  (8 shorter events, 0.0 us)
Async XLA Ops:
  6.5 242.1 %copy-start = (bf16[3,2,512,256]{3,2,1,0:T(8,128)(2,1)S(1)}, bf16[3,2,512,256]{3,2,1,0:T(8,128)(2,1)}, u32[]{:S(2)}) copy-start(bf16[3,2,512,256]{3,2,1,0:T(8,128)(2,1)} %param.9) | copy-start | bytes 4718596
  6.5 21.2 %copy-start.2 = (s32[48]{0:T(128)S(1)}, s32[48]{0:T(128)}, u32[]{:S(2)}) copy-start(s32[48]{0:T(128)} %param.7) | copy-start | bytes 580
  6.5 21.3 %copy-start.3 = (s32[1,1,32]{2,1,0:T(1,128)S(1)}, s32[1,1,32]{2,1,0:T(1,128)}, u32[]{:S(2)}) copy-start(s32[1,1,32]{2,1,0:T(1,128)} %param.6) | copy-start | bytes 388
  6.5 424.3 %all-gather.3.cloned.1.call-start = ((), (), s32[]{:S(2)}) async-start(), calls=%async_computation.1 | async-start | bytes 14155776 | tf_op jit(solution)/shard_map/all_gather | solution.py:35
  430.9 9.3 %copy-start.1 = (bf16[3,2,512,256]{3,2,1,0:T(8,128)(2,1)S(1)}, bf16[3,2,512,256]{3,2,1,0:T(8,128)(2,1)}, u32[]{:S(2)}) copy-start(bf16[3,2,512,256]{3,2,1,0:T(8,128)(2,1)} %param.9) | copy-start | bytes 4718596
Sparse Core Ops, SparseCore 0:
  286.1 144.7 all-gather.2
